TPU v7x, 512 devices: a whole 4x4x16 slice. The times are simulated.
512 devices in a mesh: grp: 16 (over y_lo, x, core), mem: 32 (over y_hi, z).
Axes of the slice: x: 4, y: 4 (y_hi: 2, y_lo: 2; y = y_hi * 2 + y_lo), z: 16, core: 2. Of those that a mesh axis runs over, the one named last changes fastest.
Arguments:
- features: float32 [12288, 256], P('mem'), may hold values from -6 to 6
- patterns: bfloat16 [16, 32, 32, 2, 128, 128], P('grp', 'mem'), may hold values from 0 to 2, as said below
- src_tile: int32 [16, 32, 32, 2], P('grp', 'mem'), may hold values from 0 to 2
- dst_tile: int32 [16, 32, 32, 2], P('grp', 'mem'), may hold values from 0 to 2
- tile_count: int32 [16, 32], P('grp', 'mem'), may hold values from 16 to 64, as said below
- cotangent: float32 [12288, 256], P(('mem', 'grp')), may hold values from -6 to 6
- w_self: float32 [256, 256], replicated, may hold values from -0.375 to 0.375
- w_neigh: float32 [256, 256], replicated, may hold values from -0.375 to 0.375
- bias: float32 [256], replicated, may hold values from -3 to 3
Outputs:
- layer_out: float32 [12288, 256], P(('mem', 'grp'))
- grad_self: float32 [256, 256], replicated
- grad_neigh: float32 [256, 256], replicated
- grad_bias: float32 [256], replicated
Inputs may be any that keep to these rules, and one draw needn't show every extreme that they name: `tile_count`: some group has all 64 slots live for some destination block. `patterns`: edge weights are zero or positive.
All inputs are finite; a program needn't handle non-finite values.
Results may differ from a plain program's by a relative error of at most 0.0003.
Values sent between devices are 32-bit elements; how exact they have to be, the bound alone decides.
A program may use at most 64 MiB of HBM per device.

v0:
```python
import jax
import jax.numpy as jnp
from jax import lax
from jax.sharding import PartitionSpec as P


def accumulate(masks, place, rows):
    contrib = jnp.einsum("jpab,jpbd->jpad", masks, rows, precision=lax.Precision.HIGHEST)
    return jnp.einsum("jpt,jpad->tad", place, contrib, precision=lax.Precision.HIGHEST)


def finish(summed, degree, own, cotangent, w_self, w_neigh, bias):
    neigh = summed / jnp.sqrt(1.0 + degree)[:, None]
    pre = jnp.dot(own, w_self, precision=lax.Precision.HIGHEST, preferred_element_type=jnp.float32)
    pre = (
        pre
        + jnp.dot(
            neigh, w_neigh, precision=lax.Precision.HIGHEST, preferred_element_type=jnp.float32
        )
        + bias
    )
    sig = jax.nn.sigmoid(pre)
    layer_out = pre * sig
    dpre = cotangent * sig * (1.0 + pre * (1.0 - sig))
    grad_self = jnp.dot(
        own.T, dpre, precision=lax.Precision.HIGHEST, preferred_element_type=jnp.float32
    )
    grad_neigh = jnp.dot(
        neigh.T, dpre, precision=lax.Precision.HIGHEST, preferred_element_type=jnp.float32
    )
    return (layer_out, grad_self, grad_neigh, jnp.sum(dpre, axis=0))


def on_device(features, patterns, src_tile, dst_tile, tile_count, cotangent, w_self, w_neigh, bias):
    weights = patterns[0, 0]
    sources = src_tile[0, 0]
    targets = dst_tile[0, 0]
    tile = weights.shape[2]
    members = weights.shape[0]
    slots = weights.shape[1]
    block = features.shape[0]
    width = features.shape[1]
    tblocks = block // tile
    order = jnp.arange(members)[:, None] * slots + jnp.arange(slots)[None, :]
    live = (order < tile_count[0, 0]).astype(jnp.float32)
    place = (targets[..., None] == jnp.arange(tblocks)).astype(jnp.float32) * live[..., None]
    masks = weights.astype(jnp.float32)
    degree = jnp.einsum(
        "jpt,jpa->ta", place, jnp.sum(masks, axis=3), precision=lax.Precision.HIGHEST
    ).reshape(block)
    piece = lax.all_gather(features, "mem", axis=0, tiled=True)
    shards = piece.shape[0] // block
    stacked = piece.reshape(shards * tblocks, tile, width)
    picked = jnp.arange(shards)[:, None] * tblocks + sources
    summed = accumulate(masks, place, stacked[picked])
    summed = summed.reshape(block, width)
    share = cotangent.shape[0]
    offset = lax.axis_index("grp") * share
    own = lax.dynamic_slice_in_dim(features, offset, share, 0)
    part_sum, part_degree = (
        lax.psum_scatter(summed, "grp", scatter_dimension=0, tiled=True),
        lax.psum_scatter(degree, "grp", scatter_dimension=0, tiled=True),
    )
    layer_out, grad_self, grad_neigh, grad_bias = finish(
        part_sum, part_degree, own, cotangent, w_self, w_neigh, bias
    )
    grad_self, grad_neigh, grad_bias = lax.psum((grad_self, grad_neigh, grad_bias), ("grp", "mem"))
    return (layer_out, grad_self, grad_neigh, grad_bias)


def solution(mesh):
    placed = (
        P("mem", None),
        P("grp", "mem", None, None, None, None),
        P("grp", "mem", None, None),
        P("grp", "mem", None, None),
        P("grp", "mem"),
        P(("mem", "grp"), None),
        P(),
        P(),
        P(),
    )
    return jax.shard_map(
        on_device,
        mesh=mesh,
        in_specs=placed,
        out_specs=(P(("mem", "grp"), None), P(), P(), P()),
        check_vma=False,
    )
```

profile of v0, /device:TPU:1, one launch (start us, length us, event | category | flops | bytes accessed | tf_op | source)
XLA Modules:
  0.0 824.0 jit_solution(17553899040861458311)
XLA Ops:
  7.2 0.0 copy-start
  7.2 0.0 all-gather.2.cloned.1.call-start
  7.2 0.7 all-gather.2.cloned.1.call-update
  7.9 0.0 reduce-scatter.2.cloned.1.call-start
  8.6 0.7 compare_select_fusion
  9.3 0.1 copy.16
  9.4 0.1 reshape.97
  9.5 227.4 %all-gather.2.cloned.1.call-done = f32[12288,256]{1,0:T(8,128)} async-done(((f32[384,256]{1,0:T(8,128)}), f32[12288,256]{1,0:T(8,128)}) %all-gather.2.cloned.1.call-update) | async-done | bytes 12582928 | tf_op jit(solution)/shard_map/all_gather | solution.py:51
  236.9 0.0 copy-start.1
  236.9 9.0 %gather_fusion = f32[64,128,256]{2,1,0:T(8,128)} fusion(f32[96,128,256]{2,1,0:T(8,128)} %bitcast.37, s32[1024]{0:T(1024)S(1)} %pad_clamp_fusion), kind=kCustom, calls=%fused_computation | custom fusion | bytes 16777472 | tf_op jit(solution)/shard_map/gather | solution.py:55
  246.0 0.0 copy-done.1
  246.0 11.7 %convolution_bitcast_fusion = f32[32,2,128,256]{2,3,1,0:T(8,128)} fusion(f32[32,2,128,256]{3,2,1,0:T(8,128)} %bitcast.36, bf16[1,1,32,2,128,128]{5,4,3,2,1,0:T(8,128)(2,1)S(1)} %copy-done.1), kind=kOutput, calls=%fused_computation.2 | convolution fusion | flops 3221225472 | bytes 18874368 | tf_op jit(solution)/shard_map/jpab,jpbd->jpad/dot_general | solution.py:8
  257.6 0.0 copy-start.4
  257.7 10.4 %copy.18 = f32[32,2,128,256]{3,0,1,2:T(8,128)} copy(f32[32,2,128,256]{2,3,1,0:T(8,128)} %convolution_bitcast_fusion) | data formatting | bytes 16777216 | tf_op jit(solution)/shard_map/jpab,jpbd->jpad/dot_general | solution.py:8
  268.0 0.0 copy-start.2
  268.0 0.0 copy-start.3
  268.0 0.0 copy-start.5
  268.0 0.0 copy-done.4
  268.0 6.6 convolution_bitcast_fusion.1
  274.6 0.8 copy.19
  275.4 0.0 reduce-scatter.2.cloned.1.call-update
  275.4 0.0 all-reduce.4.cloned.1.call-start
  275.5 1.3 dynamic-slice
  277.4 0.6 convert_reduce_fusion
  278.1 0.2 convolution_bitcast_fusion.2
  278.3 31.2 %all-reduce = f32[384]{0:T(512)S(1)} all-reduce(f32[384]{0:T(512)S(1)} %convolution_bitcast_fusion.2), channel_id=3, replica_groups=mesh['grp'=16,'mem'=32] {'grp'}, use_global_device_ids=true, to_apply=%region_2.0.clone | all-reduce | flops 384 | bytes 3072
  309.5 0.1 fusion.16
  309.6 0.0 copy-done.2
  309.6 1.0 fusion.6
  310.5 30.5 %reduce-scatter.2.cloned.1.call-done = f32[24,256]{1,0:T(8,128)} async-done(((f32[384,256]{1,0:T(8,128)}), f32[24,256]{1,0:T(8,128)}) %reduce-scatter.2.cloned.1.call-update) | async-done | bytes 24592 | tf_op jit(solution)/shard_map/reduce_scatter | solution.py:61
  341.0 0.0 copy-done
  341.0 0.0 copy-done.3
  341.0 0.0 copy-done.5
  341.0 1.6 fusion.21
  342.7 1.9 fusion.4
  344.5 1.9 fusion.9
  346.4 0.0 all-reduce.4.cloned.1.call-update
  346.5 106.5 %psum.23 = f32[256]{0:T(256)} all-reduce(f32[256]{0:T(256)S(1)} %get-tuple-element.6), channel_id=1, replica_groups=mesh['grp'=16,'mem'=32] {'grp','mem'}, use_global_device_ids=true, to_apply=%region_6.0 | all-reduce | flops 256 | bytes 2048 | tf_op jit(solution)/shard_map/psum | solution.py:67
  452.9 361.2 %all-reduce.4.cloned.1.call-done = (f32[256,256]{1,0:T(8,128)}, f32[256,256]{1,0:T(8,128)}) async-done(((f32[256,256]{1,0:T(8,128)}, f32[256,256]{1,0:T(8,128)}), (f32[256,256]{1,0:T(8,128)}, f32[256,256]{1,0:T(8,128)})) %all-reduce.4.cloned.1.call-update) | async-done | bytes 524304 | tf_op jit(solution)/shard_map/psum | solution.py:67
  814.1 1.7 copy.27
  815.8 1.7 copy.28
  (4 shorter events, 0.0 us)
Async XLA Ops:
  7.2 333.9 %copy-start = (f32[256,256]{1,0:T(8,128)S(1)}, f32[256,256]{1,0:T(8,128)}, u32[]{:S(2)}) copy-start(f32[256,256]{1,0:T(8,128)} %param.16) | copy-start | bytes 786436
  7.2 229.8 %all-gather.2.cloned.1.call-start = ((), (), s32[]{:S(2)}) async-start(), calls=%async_computation.1 | async-start | bytes 12976128 | tf_op jit(solution)/shard_map/all_gather | solution.py:51
  7.9 333.1 %reduce-scatter.2.cloned.1.call-start = ((), (), s32[]{:S(2)}) async-start(), calls=%async_computation.2 | async-start | bytes 417792 | tf_op jit(solution)/shard_map/reduce_scatter | solution.py:61
  236.9 9.0 %copy-start.1 = (bf16[1,1,32,2,128,128]{5,4,3,2,1,0:T(8,128)(2,1)S(1)}, bf16[1,1,32,2,128,128]{5,4,3,2,1,0:T(8,128)(2,1)}, u32[]{:S(2)}) copy-start(bf16[1,1,32,2,128,128]{5,4,3,2,1,0:T(8,128)(2,1)} %param.10) | copy-start | bytes 6291460
  257.6 10.4 %copy-start.4 = (s32[1,1,32,2]{2,3,1,0:T(2,128)S(1)}, s32[1,1,32,2]{2,3,1,0:T(2,128)}, u32[]{:S(2)}) copy-start(s32[1,1,32,2]{2,3,1,0:T(2,128)} %param.12) | copy-start | bytes 772
  268.0 41.5 %copy-start.2 = (f32[256,256]{1,0:T(8,128)S(1)}, f32[256,256]{1,0:T(8,128)}, u32[]{:S(2)}) copy-start(f32[256,256]{1,0:T(8,128)} %param.15) | copy-start | bytes 786436
  268.0 73.0 %copy-start.3 = (f32[24,256]{1,0:T(8,128)S(1)}, f32[24,256]{1,0:T(8,128)}, u32[]{:S(2)}) copy-start(f32[24,256]{1,0:T(8,128)} %param.14) | copy-start | bytes 73732
  268.0 73.0 %copy-start.5 = (f32[256]{0:T(256)S(1)}, f32[256]{0:T(256)}, u32[]{:S(2)}) copy-start(f32[256]{0:T(256)} %param.17) | copy-start | bytes 3076
  275.4 538.7 %all-reduce.4.cloned.1.call-start = ((), (), s32[]{:S(2)}) async-start(), calls=%async_computation.3 | async-start | bytes 1048576 | tf_op jit(solution)/shard_map/psum | solution.py:67
Sparse Core Ops, SparseCore 0:
  11.1 225.7 all-gather.1
  275.5 65.4 reduce-scatter.1
  347.1 466.9 all-reduce.3
where the time goes:
time: 825 us; the launch traced here: 824 us
  waiting for transfers between devices  620 us (75%)
  blocking collectives  138 us (17%)
  local copies, waits for them, and re-layouts  25 us (3%)
  matrix products  24.9 us (3%)
  between operations  15.1 us (2%)
    psum x1, waiting for transfers between devices, on_device(): lax.psum((grad_self, grad_neigh, grad_bias), ('grp', 'mem'))  361 us
    all_gather x1, waiting for transfers between devices, on_device(): piece = lax.all_gather(features, 'mem', axis=0, tiled=True)  227 us
    psum x1, blocking collectives, on_device(): lax.psum((grad_self, grad_neigh, grad_bias), ('grp', 'mem'))  106 us
    unnamed x1, blocking collectives  31.2 us
    reduce_scatter x1, waiting for transfers between devices, on_device(): lax.psum_scatter(summed, 'grp', scatter_dimension=0, tiled=True)  30.5 us
  transfers between devices with their start and end apart: 3, of which 3 were waited for; matrix products, arithmetic and copies ran while one was open for 0% of the time, Pallas kernels for 0%

commit v1 on v0

v1 whole, which is shorter than its diff:
```python
import jax
import jax.numpy as jnp
from jax import lax
from jax.experimental import pallas as pl
from jax.experimental.pallas import tpu as pltpu
from jax.sharding import PartitionSpec as P

MESH = pl.DeviceIdType.MESH
HIGH = lax.Precision.HIGHEST
F32 = jnp.float32
NX, NY, NZ = 4, 4, 16
GRP, MEM = 16, 32
TILES = 9


def remote(src, dst, send, recv, dev):
    return pltpu.make_async_remote_copy(
        src_ref=src, dst_ref=dst, send_sem=send, recv_sem=recv, device_id=dev, device_id_type=MESH
    )


def gather_kernel(f_ref, g_ref, zs, zr, ys, yr, ws, wr, xs, xr, cs, cr, own_sem):
    g = lax.axis_index("grp")
    m = lax.axis_index("mem")
    core = g % 2
    x = (g // 2) % NX
    y = (m // NZ) * 2 + g // (2 * NX)
    z = m % NZ
    xp = x % 2

    def dev(x_, y_, z_, c_):
        return ((y_ % 2) * NX + x_) * 2 + c_, (y_ // 2) * NZ + z_

    right_z, left_z = (z + 1) % NZ, (z + NZ - 1) % NZ
    right_y, left_y = (y + 1) % NY, (y + NY - 1) % NY
    right_x, left_x = (x + 1) % NX, (x + NX - 1) % NX
    across_y = (y + 2) % NY

    peers = (
        dev(x, y, right_z, core), dev(x, y, left_z, core),
        dev(x, right_y, z, core), dev(x, left_y, z, core),
        dev(right_x, y, z, core), dev(left_x, y, z, core),
        dev(x, y, z, 1 - core),
    )
    barrier = pltpu.get_barrier_semaphore()
    for peer in peers:
        pl.semaphore_signal(barrier, inc=1, device_id=peer, device_id_type=MESH)
    pl.semaphore_wait(barrier, len(peers))

    def z_of(q):
        t = (q + 1) // 2
        return jnp.where(q % 2 == 1, z + NZ - t, z + t) % NZ

    def piece(q, y_):
        return g_ref.at[z_of(q), core, xp, :, y_]

    own = f_ref.at[core, xp, :, y % 2]
    local = pltpu.make_async_copy(own, piece(0, y), own_sem)
    local.start()
    local.wait()

    def z_copy(q, to, slot):
        return remote(piece(q, y), piece(q, y), zs.at[slot], zr.at[slot], dev(x, y, to, core))

    def near(q, side):
        to = right_y if side == 0 else left_y
        return remote(piece(q, y), piece(q, y), ys.at[q, side], yr.at[q, side], dev(x, to, z, core))

    def far(q, side):
        came, to = (left_y, right_y) if side == 0 else (right_y, left_y)
        part = g_ref.at[z_of(q), core, xp, side, came]
        return remote(part, part, ws.at[q, side], wr.at[q, side], dev(x, to, z, core))

    def cross(q, side):
        to = right_x if side == 0 else left_x
        part = g_ref.at[z_of(q), core, xp, side]
        return remote(part, part, xs.at[q, side], xr.at[q, side], dev(to, y, z, core))

    def swap(q):
        part = g_ref.at[z_of(q), core]
        return remote(part, part, cs.at[q], cr.at[q], dev(x, y, z, 1 - core))

    def step(i, carry):
        @pl.when(i < NZ)
        def _():
            q = i

            @pl.when(q == 0)
            def _():
                z_copy(q, right_z, 1).start()
                z_copy(q, left_z, 2).start()

            @pl.when(q > 0)
            def _():
                z_copy(q, right_z, q).wait_recv()

                @pl.when(q + 2 < NZ)
                def _():
                    z_copy(q, jnp.where(q % 2 == 1, right_z, left_z), q + 2).start()

            near(q, 0).start()
            near(q, 1).start()

        @pl.when((i >= 1) & (i < NZ + 1))
        def _():
            q = i - 1
            near(q, 0).wait_recv()
            far(q, 0).start()
            near(q, 1).wait_recv()
            far(q, 1).start()

        @pl.when((i >= 2) & (i < NZ + 2))
        def _():
            q = i - 2
            far(q, 0).wait_recv()
            cross(q, 0).start()
            far(q, 1).wait_recv()
            cross(q, 1).start()

        @pl.when((i >= 3) & (i < NZ + 3))
        def _():
            q = i - 3
            cross(q, 0).wait_recv()
            cross(q, 1).wait_recv()
            swap(q).start()

        return carry

    lax.fori_loop(0, NZ + 3, step, 0)

    def drain(q, carry):
        @pl.when(q > 0)
        def _():
            z_copy(q, right_z, q).wait_send()

        for side in range(2):
            near(q, side).wait_send()
            far(q, side).wait_send()
            cross(q, side).wait_send()
        swap(q).wait_send()
        swap(q).wait_recv()
        return carry

    lax.fori_loop(0, NZ, drain, 0)


def gather_all(features):
    block, width = features.shape
    rows = block // 16
    view = features.reshape(2, 2, 2, 2, rows, width)
    dma = pltpu.SemaphoreType.DMA
    return pl.pallas_call(
        gather_kernel,
        out_shape=jax.ShapeDtypeStruct((NZ, 2, 2, 2, NY, rows, width), F32),
        in_specs=[pl.BlockSpec(memory_space=pltpu.VMEM)],
        out_specs=pl.BlockSpec(memory_space=pl.ANY),
        scratch_shapes=[
            dma((NZ,)), dma((NZ,)),
            dma((NZ, 2)), dma((NZ, 2)),
            dma((NZ, 2)), dma((NZ, 2)),
            dma((NZ, 2)), dma((NZ, 2)),
            dma((NZ,)), dma((NZ,)),
            dma(()),
        ],
        compiler_params=pltpu.CompilerParams(collective_id=0, has_side_effects=True),
    )(view)


def spread_kernel(src_ref, dst_ref, cnt_ref, w_ref, f_ref, out_ref, hi_ref, lo_ref):
    z = pl.program_id(0)

    @pl.when(z == 0)
    def _():
        out_ref[...] = jnp.zeros_like(out_ref)

    tile = w_ref.shape[-1]
    width = f_ref.shape[-1]
    block = hi_ref.shape[1]
    slots = w_ref.shape[2]
    for yhi in range(2):
        full = f_ref[0, :, yhi].reshape(block, width)
        hi = full.astype(jnp.bfloat16)
        hi_ref[yhi] = hi
        lo_ref[yhi] = (full - hi.astype(F32)).astype(jnp.bfloat16)
    for yhi in range(2):
        for p in range(slots):
            order = (yhi * NZ + z) * slots + p

            @pl.when(order < cnt_ref[0])
            def _():
                take = pl.ds(pl.multiple_of(src_ref[order] * tile, tile), tile)
                give = pl.ds(pl.multiple_of(dst_ref[order] * tile, tile), tile)
                mask = w_ref[yhi, 0, p]
                part = jnp.dot(mask, hi_ref[yhi, take, :], preferred_element_type=F32)
                part += jnp.dot(mask, lo_ref[yhi, take, :], preferred_element_type=F32)
                out_ref[give, :width] += part
                out_ref[give, width:] += mask.astype(F32)


def spread(weights, gathered, sources, targets, count):
    members, slots, tile, _ = weights.shape
    rows, width = gathered.shape[-2:]
    block = 16 * rows
    view = gathered.reshape(NZ, 8, 2, 2 * rows, width)
    return pl.pallas_call(
        spread_kernel,
        out_shape=jax.ShapeDtypeStruct((block, width + tile), F32),
        grid_spec=pltpu.PrefetchScalarGridSpec(
            num_scalar_prefetch=3,
            grid=(NZ,),
            in_specs=[
                pl.BlockSpec((2, 1, slots, tile, tile), lambda z, *_: (0, z, 0, 0, 0)),
                pl.BlockSpec((1, 8, 2, 2 * rows, width), lambda z, *_: (z, 0, 0, 0, 0)),
            ],
            out_specs=pl.BlockSpec((block, width + tile), lambda z, *_: (0, 0)),
            scratch_shapes=[
                pltpu.VMEM((2, block, width), jnp.bfloat16),
                pltpu.VMEM((2, block, width), jnp.bfloat16),
            ],
        ),
        compiler_params=pltpu.CompilerParams(dimension_semantics=("arbitrary",)),
    )(
        sources.reshape(members * slots),
        targets.reshape(members * slots),
        count.reshape(1),
        weights.reshape(2, NZ, slots, tile, tile),
        view,
    )


def owner_of(k):
    return (k % 2) * NZ + (k // 2) * 3


def tail_kernel(
    u_ref, f_ref, cot_ref, ws_ref, wn_ref, b_ref,
    layer_ref, grad_ref, bias_ref,
    r1, part, r2, mine, r3, total, fin,
    s1, q1, s2, q2, s3, q3, s4, q4, s5, q5,
):
    g = lax.axis_index("grp")
    m = lax.axis_index("mem")
    width = f_ref.shape[-1]

    barrier = pltpu.get_barrier_semaphore()

    def greet_grp(k, carry):
        pl.semaphore_signal(barrier, inc=1, device_id=((g + k) % GRP, m), device_id_type=MESH)
        return carry

    def greet_mem(k, carry):
        pl.semaphore_signal(barrier, inc=1, device_id=(g, (m + k) % MEM), device_id_type=MESH)
        return carry

    lax.fori_loop(1, GRP, greet_grp, 0)
    lax.fori_loop(1, MEM, greet_mem, 0)
    pl.semaphore_wait(barrier, GRP + MEM - 2)

    def over_grp(make):
        def begin(k, carry):
            make(k).start()
            return carry

        lax.fori_loop(1, GRP, begin, 0)

    def end_grp(make):
        def end(k, carry):
            make(k).wait()
            return carry

        lax.fori_loop(1, GRP, end, 0)

    def send_sum(k):
        peer = (g + k) % GRP
        return remote(u_ref.at[peer], r1.at[k], s1.at[k], q1.at[k], (peer, m))

    over_grp(send_sum)
    own = f_ref[g]
    pre = jnp.dot(own, ws_ref[...], precision=HIGH, preferred_element_type=F32) + b_ref[...]
    end_grp(send_sum)
    whole = u_ref[g]
    for k in range(1, GRP):
        whole = whole + r1[k]
    degree = jnp.sum(whole[:, width:], axis=1, keepdims=True)
    neigh = whole[:, :width] / jnp.sqrt(1.0 + degree)
    pre = pre + jnp.dot(neigh, wn_ref[...], precision=HIGH, preferred_element_type=F32)
    sig = jax.nn.sigmoid(pre)
    layer_ref[...] = pre * sig
    dpre = cot_ref[...] * sig * (1.0 + pre * (1.0 - sig))
    dims = (((0,), (0,)), ((), ()))
    halves = (own, neigh)
    for n in range(2):
        grad = lax.dot_general(halves[n], dpre, dims, precision=HIGH, preferred_element_type=F32)
        for k in range(8):
            for t in range(8):
                low, col = k * 32 + (t // 2) * 8, (t % 2) * 128
                part[n * 8 + k, t] = grad[low : low + 8, col : col + 128]
    sums = jnp.sum(dpre, axis=0, keepdims=True)
    line = lax.broadcasted_iota(jnp.int32, (8, 128), 0)
    first = jnp.broadcast_to(sums[:, :128], (8, 128))
    second = jnp.broadcast_to(sums[:, 128:], (8, 128))
    bias_tile = jnp.where(line == 0, first, jnp.where(line == 1, second, 0.0))
    for k in range(GRP):
        part[k, 8] = bias_tile

    def send_part(k):
        peer = (g + k) % GRP
        return remote(part.at[peer], r2.at[k], s2.at[k], q2.at[k], (peer, m))

    over_grp(send_part)
    end_grp(send_part)
    acc = part[g]
    for k in range(1, GRP):
        acc = acc + r2[k]
    mine[...] = acc

    def send_tile(k):
        to = owner_of(k)
        away = (to - m + MEM) % MEM
        return remote(mine.at[k], r3.at[away], s3.at[k], q3.at[away], (g, to))

    def start_tile(k, carry):
        @pl.when(owner_of(k) != m)
        def _():
            send_tile(k).start()

        return carry

    lax.fori_loop(0, TILES, start_tile, 0)
    zz = m % NZ
    mine_k = (zz // 3) * 2 + m // NZ
    is_owner = (zz % 3 == 0) & (mine_k < TILES)

    def hand_out(k):
        return remote(total, fin.at[mine_k], s4.at[k], q4.at[mine_k], (g, (m + k) % MEM))

    @pl.when(is_owner)
    def _():
        def arrive(k, carry):
            remote(mine.at[0], r3.at[k], s3.at[0], q3.at[k], (g, (m + k) % MEM)).wait_recv()
            return carry

        lax.fori_loop(1, MEM, arrive, 0)
        acc = mine[mine_k]
        for k in range(1, MEM):
            acc = acc + r3[k]
        total[...] = acc
        fin[mine_k] = acc

        def give(k, carry):
            hand_out(k).start()
            return carry

        lax.fori_loop(1, MEM, give, 0)

    def take_tile(k, carry):
        @pl.when(owner_of(k) != m)
        def _():
            remote(total, fin.at[k], s4.at[0], q4.at[k], (g, owner_of(k))).wait_recv()
            send_tile(k).wait_send()

        return carry

    lax.fori_loop(0, TILES, take_tile, 0)

    def send_fin(k):
        peer = (g + k) % GRP
        return remote(fin.at[pl.ds(0, 8)], grad_ref.at[g], s5.at[k], q5.at[k], (peer, m))

    def recv_fin(k):
        peer = (g + GRP - k) % GRP
        return remote(fin.at[pl.ds(0, 8)], grad_ref.at[peer], s5.at[k], q5.at[k], (peer, m))

    over_grp(send_fin)
    grad_ref[g] = fin[0:8]
    bias_ref[...] = fin[8]

    def finish(k, carry):
        send_fin(k).wait_send()
        recv_fin(k).wait_recv()
        return carry

    lax.fori_loop(1, GRP, finish, 0)

    @pl.when(is_owner)
    def _():
        def done(k, carry):
            hand_out(k).wait_send()
            return carry

        lax.fori_loop(1, MEM, done, 0)


def tail(parts, features, cotangent, w_self, w_neigh, bias):
    block, width = features.shape
    share = cotangent.shape[0]
    wide = parts.shape[1]
    dma = pltpu.SemaphoreType.DMA
    vmem = pl.BlockSpec(memory_space=pltpu.VMEM)
    layer, grads, bias_tile = pl.pallas_call(
        tail_kernel,
        out_shape=(
            jax.ShapeDtypeStruct((share, width), F32),
            jax.ShapeDtypeStruct((GRP, 8, 8, 128), F32),
            jax.ShapeDtypeStruct((8, 128), F32),
        ),
        in_specs=[vmem] * 6,
        out_specs=(vmem, vmem, vmem),
        scratch_shapes=[
            pltpu.VMEM((GRP, share, wide), F32),
            pltpu.VMEM((GRP, TILES, 8, 128), F32),
            pltpu.VMEM((GRP, TILES, 8, 128), F32),
            pltpu.VMEM((TILES, 8, 128), F32),
            pltpu.VMEM((MEM, 8, 128), F32),
            pltpu.VMEM((8, 128), F32),
            pltpu.VMEM((TILES, 8, 128), F32),
            dma((GRP,)), dma((GRP,)),
            dma((GRP,)), dma((GRP,)),
            dma((TILES,)), dma((MEM,)),
            dma((MEM,)), dma((TILES,)),
            dma((GRP,)), dma((GRP,)),
        ],
        compiler_params=pltpu.CompilerParams(collective_id=1, has_side_effects=True),
    )(
        parts.reshape(GRP, share, wide),
        features.reshape(GRP, share, width),
        cotangent,
        w_self,
        w_neigh,
        bias.reshape(1, width),
    )
    full = grads.reshape(2, 32, 2, 8, 128).transpose(0, 1, 3, 2, 4).reshape(2, 256, 256)
    return layer, full[0], full[1], bias_tile[:2].reshape(width)


def on_device(features, patterns, src_tile, dst_tile, tile_count, cotangent, w_self, w_neigh, bias):
    gathered = gather_all(features)
    parts = spread(patterns[0, 0], gathered, src_tile, dst_tile, tile_count)
    return tail(parts, features, cotangent, w_self, w_neigh, bias)


def solution(mesh):
    placed = (
        P("mem", None),
        P("grp", "mem", None, None, None, None),
        P("grp", "mem", None, None),
        P("grp", "mem", None, None),
        P("grp", "mem"),
        P(("mem", "grp"), None),
        P(),
        P(),
        P(),
    )
    return jax.shard_map(
        on_device,
        mesh=mesh,
        in_specs=placed,
        out_specs=(P(("mem", "grp"), None), P(), P(), P()),
        check_vma=False,
    )
```

time: 825 us -> 162 us (0.20)
  waiting for transfers between devices: 620 us -> 0 us
  Pallas kernels: 0 us -> 153 us
  blocking collectives: 138 us -> 0 us
  matrix products: 24.9 us -> 0 us
  local copies, waits for them, and re-layouts: 25 us -> 7.2 us
  between operations: 15.1 us -> 1.3 us
    psum x1 -> x0, waiting for transfers between devices: 361 us -> none  [on_device(): lax.psum((grad_self, grad_neigh, grad_bias), ('grp', 'mem'))]
    all_gather x1 -> x0, waiting for transfers between devices: 227 us -> none  [on_device(): piece = lax.all_gather(features, 'mem', axis=0, tiled=True)]
    pallas_call x0 -> x3, Pallas kernels: none -> 153 us  [the longest x1 79.3 us: gather_all(): pl.pallas_call(gather_kernel, out_shape=jax.ShapeDtypeStruct((NZ, 2, 2, 2...]
    psum x1 -> x0, blocking collectives: 106 us -> none  [on_device(): lax.psum((grad_self, grad_neigh, grad_bias), ('grp', 'mem'))]
    unnamed x1 -> x0, blocking collectives: 31.2 us -> none
    reduce_scatter x1 -> x0, waiting for transfers between devices: 30.5 us -> none  [on_device(): lax.psum_scatter(summed, 'grp', scatter_dimension=0, tiled=True)]
    dot_general x7 -> x0, matrix products: 24.9 us -> none  [the longest x1 11.7 us: accumulate(): jnp.einsum('jpab,jpbd->jpad', masks, rows, precision=lax.Precision.HIGHEST)]
    dot_general x2 -> x0, local copies, waits for them, and re-layouts: 11.2 us -> none  [the longest x1 10.4 us: accumulate(): jnp.einsum('jpab,jpbd->jpad', masks, rows, precision=lax.Precision.HIGHEST)]
  transfers between devices with their start and end apart: 3 -> 0, of which waited for: 3 -> 0; matrix products, arithmetic and copies ran while one was open for 0% -> 0% of each run, Pallas kernels for 0% -> 0%
where the time goes in v1:
time: 162 us; the launch traced here: 161 us
  Pallas kernels  153 us (94%)
  local copies, waits for them, and re-layouts  7.2 us (4%)
    pallas_call x1, Pallas kernels, gather_all(): pl.pallas_call(gather_kernel, out_shape=jax.ShapeDtypeStruct((NZ, 2, 2, 2...  79.3 us
    pallas_call x1, Pallas kernels, tail(): pl.pallas_call(tail_kernel, out_shape=(jax.ShapeDtypeStruct((share, width...  56.6 us
    pallas_call x1, Pallas kernels, spread(): pl.pallas_call(spread_kernel, out_shape=jax.ShapeDtypeStruct((block, widt...  16.8 us

profile of v1, /device:TPU:1, one launch (start us, length us, event | category | flops | bytes accessed | tf_op | source)
XLA Modules:
  0.0 161.2 jit_solution(4486802866158303958)
XLA Ops:
  1.3 0.8 copy.15
  2.0 0.6 reshape.43.src_ref
  2.7 0.8 copy.16
  3.4 0.6 reshape.44.dst_ref
  4.0 79.3 %shard_map.120 = f32[16,2,2,2,4,24,256]{6,5,4,3,2,1,0:T(8,128)} custom-call(f32[2,2,2,2,24,256]{5,4,3,2,1,0:T(8,128)} %bitcast.24), custom_call_target="tpu_custom_call" | custom-call | tf_op jit(solution)/shard_map/pallas_call | solution.py:152
  83.4 16.8 %shard_map.121 = f32[384,384]{1,0:T(8,128)} custom-call(s32[64]{0:T(128)} %reshape.43.src_ref, s32[64]{0:T(128)} %reshape.44.dst_ref, s32[1]{0:T(128)} %bitcast.20.cnt_ref, bf16[2,16,2,128,128]{4,3,2,1,0:T(8,128)(2,1)} %bitcast.23, f32[16,8,2,48,256]{4,3,2,1,0:T(8,128)} %bitcast.21), custom_call_target="tpu_custom_call" | custom-call | tf_op jit(solution)/shard_map/pallas_call | solution.py:205
  100.2 56.6 %shard_map.122 = (f32[24,256]{1,0:T(8,128)}, f32[16,8,8,128]{3,2,1,0:T(8,128)}, f32[8,128]{1,0:T(8,128)}) custom-call(f32[16,24,384]{2,1,0:T(8,128)} %bitcast.22, f32[16,24,256]{2,1,0:T(8,128)} %bitcast.25, f32[24,256]{1,0:T(8,128)} %cot_ref.1, f32[256,256]{1,0:T(8,128)} %ws_ref.1, f32[256,256]{1,0:T(8,128)} %wn_ref.1, f32[1,256]{1,0:T(1,128)} %bitcast.27), custom_call_target="tpu_custom_call" | custom-call | tf_op jit(solution)/shard_map/pallas_call | solution.py:400
  156.7 1.9 %slice_bitcast_fusion = (f32[256,256]{1,0:T(8,128)}, f32[256,256]{1,0:T(8,128)}) fusion(f32[2,32,8,2,128]{4,2,3,1,0:T(8,128)} %bitcast.26), kind=kLoop, calls=%fused_computation | loop fusion | bytes 1048576 | tf_op jit(solution)/shard_map/squeeze | solution.py:433
  158.6 1.2 slice_bitcast_fusion.2
  159.8 1.3 copy.19

commit v2 on v1

v2 whole, which is shorter than its diff:
```python
import jax
import jax.numpy as jnp
from jax import lax
from jax.experimental import pallas as pl
from jax.experimental.pallas import tpu as pltpu
from jax.sharding import PartitionSpec as P

MESH = pl.DeviceIdType.MESH
HIGH = lax.Precision.HIGHEST
F32 = jnp.float32
NX, NY, NZ = 4, 4, 16
GRP, MEM = 16, 32
TILES = 9
LAG = 2


def remote(src, dst, send, recv, dev):
    return pltpu.make_async_remote_copy(
        src_ref=src, dst_ref=dst, send_sem=send, recv_sem=recv, device_id=dev, device_id_type=MESH
    )


def owner_of(k):
    return (k % 2) * NZ + (k // 2) * 3


def kernel(
    src_ref, dst_ref, cnt_ref, f_ref, w_ref, cot_ref, ws_ref, wn_ref, b_ref,
    layer_ref, grad_ref, bias_ref,
    g_ref, pair_ref, acc_ref, deg_ref, u_ref, r1, part, r2, mine, r3, total, fin,
    zs, zr, ys, yr, fs, fr, xs, xr, cs, cr, own_sem,
    s1, q1, s2, q2, s3, q3, s4, q4, s5, q5,
):
    g = lax.axis_index("grp")
    m = lax.axis_index("mem")
    core = g % 2
    x = (g // 2) % NX
    y = (m // NZ) * 2 + g // (2 * NX)
    z = m % NZ
    xp = x % 2
    share, width = f_ref.shape[-2:]
    block = GRP * share
    slots, tile = w_ref.shape[2], w_ref.shape[3]
    tblocks = block // tile

    def dev(x_, y_, z_, c_):
        return ((y_ % 2) * NX + x_) * 2 + c_, (y_ // 2) * NZ + z_

    right_z, left_z = (z + 1) % NZ, (z + NZ - 1) % NZ
    right_y, left_y = (y + 1) % NY, (y + NY - 1) % NY
    right_x, left_x = (x + 1) % NX, (x + NX - 1) % NX

    barrier = pltpu.get_barrier_semaphore()

    def greet_grp(k, carry):
        pl.semaphore_signal(barrier, inc=1, device_id=((g + k) % GRP, m), device_id_type=MESH)
        return carry

    def greet_mem(k, carry):
        pl.semaphore_signal(barrier, inc=1, device_id=(g, (m + k) % MEM), device_id_type=MESH)
        return carry

    for peer in (dev(x, right_y, z, core), dev(x, left_y, z, core)):
        pl.semaphore_signal(barrier, inc=1, device_id=peer, device_id_type=MESH)
    lax.fori_loop(1, GRP, greet_grp, 0)
    lax.fori_loop(1, MEM, greet_mem, 0)
    pl.semaphore_wait(barrier, GRP + MEM)

    def z_of(q):
        t = (q + 1) // 2
        return jnp.where(q % 2 == 1, z + NZ - t, z + t) % NZ

    def piece(q, y_):
        return g_ref.at[z_of(q), core, xp, :, y_]

    own_part = f_ref.at[core, xp, :, y % 2]
    local = pltpu.make_async_copy(own_part, piece(0, y), own_sem)
    local.start()
    acc_ref[...] = jnp.zeros_like(acc_ref)
    deg_ref[...] = jnp.zeros_like(deg_ref)
    local.wait()

    def z_copy(q, to, slot):
        return remote(piece(q, y), piece(q, y), zs.at[slot], zr.at[slot], dev(x, y, to, core))

    def near(q, side):
        to = right_y if side == 0 else left_y
        return remote(piece(q, y), piece(q, y), ys.at[q, side], yr.at[q, side], dev(x, to, z, core))

    def far(q, side):
        came, to = (left_y, right_y) if side == 0 else (right_y, left_y)
        half = g_ref.at[z_of(q), core, xp, side, came]
        return remote(half, half, fs.at[q, side], fr.at[q, side], dev(x, to, z, core))

    def cross(q, side):
        to = right_x if side == 0 else left_x
        half = g_ref.at[z_of(q), core, xp, side]
        return remote(half, half, xs.at[q, side], xr.at[q, side], dev(to, y, z, core))

    def swap(q):
        half = g_ref.at[z_of(q), core]
        return remote(half, half, cs.at[q], cr.at[q], dev(x, y, z, 1 - core))

    def multiply(q):
        zq = z_of(q)
        add = None
        deg = None
        for yhi in range(2):
            rows = g_ref[zq, :, :, :, yhi * 2 : yhi * 2 + 2].reshape(block, width)
            hi = rows.astype(jnp.bfloat16)
            lo = (rows - hi.astype(F32)).astype(jnp.bfloat16)
            for s in range(tblocks):
                pair_ref[yhi, s, :tile] = hi[s * tile : (s + 1) * tile]
                pair_ref[yhi, s, tile:] = lo[s * tile : (s + 1) * tile]
        for yhi in range(2):
            j = yhi * NZ + zq
            for p in range(slots):
                live = j * slots + p < cnt_ref[0, 0]
                mask = w_ref[yhi, zq, p].astype(F32)
                placed = jnp.concatenate(
                    [
                        mask * jnp.where(live & (dst_ref[p, j] == t), 1.0, 0.0)
                        for t in range(tblocks)
                    ],
                    axis=0,
                )
                lhs = placed.astype(jnp.bfloat16)
                both = jnp.concatenate([lhs, lhs], axis=1)
                prod = jnp.dot(both, pair_ref[yhi, src_ref[p, j]], preferred_element_type=F32)
                add = prod if add is None else add + prod
                deg = placed if deg is None else deg + placed
        acc_ref[...] += add
        deg_ref[...] += deg

    def within(i, late):
        return (i >= late) & (i < NZ + late)

    def step(i, carry):
        @pl.when(i < NZ)
        def _():
            q = i

            @pl.when(q == 0)
            def _():
                z_copy(q, right_z, 1).start()
                z_copy(q, left_z, 2).start()

            @pl.when(q > 0)
            def _():
                z_copy(q, right_z, q).wait_recv()

                @pl.when(q + 2 < NZ)
                def _():
                    z_copy(q, jnp.where(q % 2 == 1, right_z, left_z), q + 2).start()

            near(q, 0).start()
            near(q, 1).start()

        @pl.when(within(i, LAG))
        def _():
            q = i - LAG
            near(q, 0).wait_recv()
            far(q, 0).start()
            near(q, 1).wait_recv()
            far(q, 1).start()

        @pl.when(within(i, 2 * LAG))
        def _():
            q = i - 2 * LAG
            far(q, 0).wait_recv()
            cross(q, 0).start()
            far(q, 1).wait_recv()
            cross(q, 1).start()

        @pl.when(within(i, 3 * LAG))
        def _():
            q = i - 3 * LAG
            cross(q, 0).wait_recv()
            cross(q, 1).wait_recv()
            swap(q).start()

        @pl.when(within(i, 4 * LAG))
        def _():
            q = i - 4 * LAG
            swap(q).wait_recv()
            multiply(q)

        return carry

    lax.fori_loop(0, NZ + 4 * LAG, step, 0)

    line = lax.broadcasted_iota(jnp.int32, (8, 128), 0)
    ones = jnp.ones((8, tile), F32)
    lanes = lax.dot_general(
        ones, deg_ref[...], (((1,), (1,)), ((), ())), precision=HIGH, preferred_element_type=F32
    )
    deg_tile = jnp.zeros((8, tile), F32)
    for t in range(tblocks):
        deg_tile = jnp.where(line == t, lanes[:, t * tile : (t + 1) * tile], deg_tile)
    for k in range(GRP):
        u_ref[k, :share] = acc_ref[k * share : (k + 1) * share]
        u_ref[k, share:, :tile] = deg_tile
        u_ref[k, share:, tile:] = deg_tile

    def over_grp(make):
        def begin(k, carry):
            make(k).start()
            return carry

        lax.fori_loop(1, GRP, begin, 0)

    def end_grp(make):
        def end(k, carry):
            make(k).wait()
            return carry

        lax.fori_loop(1, GRP, end, 0)

    def send_sum(k):
        peer = (g + k) % GRP
        return remote(u_ref.at[peer], r1.at[k], s1.at[k], q1.at[k], (peer, m))

    over_grp(send_sum)

    def drain(q, carry):
        @pl.when(q > 0)
        def _():
            z_copy(q, right_z, q).wait_send()

        for side in range(2):
            near(q, side).wait_send()
            far(q, side).wait_send()
            cross(q, side).wait_send()
        swap(q).wait_send()
        return carry

    lax.fori_loop(0, NZ, drain, 0)
    own = f_ref[g // 8, (g // 4) % 2, (g // 2) % 2, g % 2]
    pre = jnp.dot(own, ws_ref[...], precision=HIGH, preferred_element_type=F32) + b_ref[...]
    end_grp(send_sum)
    whole = u_ref[g]
    for k in range(1, GRP):
        whole = whole + r1[k]
    at = g * share + lax.broadcasted_iota(jnp.int32, (share, tile), 0)
    lane = lax.broadcasted_iota(jnp.int32, (share, tile), 1)
    degree = jnp.zeros((share, tile), F32)
    for t in range(tblocks):
        row = jnp.broadcast_to(whole[share + t : share + t + 1, :tile], (share, tile))
        degree = jnp.where(at == t * tile + lane, row, degree)
    degree = jnp.sum(degree, axis=1, keepdims=True)
    neigh = whole[:share] / jnp.sqrt(1.0 + degree)
    pre = pre + jnp.dot(neigh, wn_ref[...], precision=HIGH, preferred_element_type=F32)
    sig = jax.nn.sigmoid(pre)
    layer_ref[...] = pre * sig
    dpre = cot_ref[...] * sig * (1.0 + pre * (1.0 - sig))
    dims = (((0,), (0,)), ((), ()))
    halves = (own, neigh)
    for n in range(2):
        grad = lax.dot_general(halves[n], dpre, dims, precision=HIGH, preferred_element_type=F32)
        for k in range(8):
            for t in range(8):
                low, col = k * 32 + (t // 2) * 8, (t % 2) * 128
                part[n * 8 + k, t] = grad[low : low + 8, col : col + 128]
    sums = jnp.sum(dpre, axis=0, keepdims=True)
    first = jnp.broadcast_to(sums[:, :128], (8, 128))
    second = jnp.broadcast_to(sums[:, 128:], (8, 128))
    bias_tile = jnp.where(line == 0, first, jnp.where(line == 1, second, 0.0))
    for k in range(GRP):
        part[k, 8] = bias_tile

    def send_part(k):
        peer = (g + k) % GRP
        return remote(part.at[peer], r2.at[k], s2.at[k], q2.at[k], (peer, m))

    over_grp(send_part)
    end_grp(send_part)
    acc = part[g]
    for k in range(1, GRP):
        acc = acc + r2[k]
    mine[...] = acc

    def send_tile(k):
        to = owner_of(k)
        away = (to - m + MEM) % MEM
        return remote(mine.at[k], r3.at[away], s3.at[k], q3.at[away], (g, to))

    def start_tile(k, carry):
        @pl.when(owner_of(k) != m)
        def _():
            send_tile(k).start()

        return carry

    lax.fori_loop(0, TILES, start_tile, 0)
    zz = m % NZ
    mine_k = (zz // 3) * 2 + m // NZ
    is_owner = (zz % 3 == 0) & (mine_k < TILES)

    def hand_out(k):
        return remote(total, fin.at[mine_k], s4.at[k], q4.at[mine_k], (g, (m + k) % MEM))

    @pl.when(is_owner)
    def _():
        def arrive(k, carry):
            remote(mine.at[0], r3.at[k], s3.at[0], q3.at[k], (g, (m + k) % MEM)).wait_recv()
            return carry

        lax.fori_loop(1, MEM, arrive, 0)
        acc = mine[mine_k]
        for k in range(1, MEM):
            acc = acc + r3[k]
        total[...] = acc
        fin[mine_k] = acc

        def give(k, carry):
            hand_out(k).start()
            return carry

        lax.fori_loop(1, MEM, give, 0)

    def take_tile(k, carry):
        @pl.when(owner_of(k) != m)
        def _():
            remote(total, fin.at[k], s4.at[0], q4.at[k], (g, owner_of(k))).wait_recv()
            send_tile(k).wait_send()

        return carry

    lax.fori_loop(0, TILES, take_tile, 0)

    def send_fin(k):
        peer = (g + k) % GRP
        return remote(fin.at[pl.ds(0, 8)], grad_ref.at[g], s5.at[k], q5.at[k], (peer, m))

    def recv_fin(k):
        peer = (g + GRP - k) % GRP
        return remote(fin.at[pl.ds(0, 8)], grad_ref.at[peer], s5.at[k], q5.at[k], (peer, m))

    over_grp(send_fin)
    grad_ref[g] = fin[0:8]
    bias_ref[...] = fin[8]

    def finish(k, carry):
        send_fin(k).wait_send()
        recv_fin(k).wait_recv()
        return carry

    lax.fori_loop(1, GRP, finish, 0)

    @pl.when(is_owner)
    def _():
        def done(k, carry):
            hand_out(k).wait_send()
            return carry

        lax.fori_loop(1, MEM, done, 0)


def pack_kernel(layer_ref, tiles_ref, bias_ref, layer_out, self_out, neigh_out, bias_out):
    layer_out[...] = layer_ref[...]
    for n, out in enumerate((self_out, neigh_out)):
        for k in range(8):
            for t in range(8):
                low, col = k * 32 + (t // 2) * 8, (t % 2) * 128
                out[low : low + 8, col : col + 128] = tiles_ref[n * 8 + k, t]
    bias_out[:, :128] = bias_ref[0:1]
    bias_out[:, 128:] = bias_ref[1:2]


def on_device(features, patterns, src_tile, dst_tile, tile_count, cotangent, w_self, w_neigh, bias):
    block, width = features.shape
    share = cotangent.shape[0]
    members, slots, tile, _ = patterns.shape[2:]
    tblocks = block // tile
    dma = pltpu.SemaphoreType.DMA
    vmem = pl.BlockSpec(memory_space=pltpu.VMEM)
    smem = pl.BlockSpec(memory_space=pltpu.SMEM)
    layer, tiles, bias_tile = pl.pallas_call(
        kernel,
        out_shape=(
            jax.ShapeDtypeStruct((share, width), F32),
            jax.ShapeDtypeStruct((GRP, 8, 8, 128), F32),
            jax.ShapeDtypeStruct((8, 128), F32),
        ),
        in_specs=[smem] * 3 + [vmem] * 6,
        out_specs=(vmem, vmem, vmem),
        scratch_shapes=[
            pltpu.VMEM((NZ, 2, 2, 2, NY, share, width), F32),
            pltpu.VMEM((2, tblocks, 2 * tile, width), jnp.bfloat16),
            pltpu.VMEM((block, width), F32),
            pltpu.VMEM((block, tile), F32),
            pltpu.VMEM((GRP, share + 8, width), F32),
            pltpu.VMEM((GRP, share + 8, width), F32),
            pltpu.VMEM((GRP, TILES, 8, 128), F32),
            pltpu.VMEM((GRP, TILES, 8, 128), F32),
            pltpu.VMEM((TILES, 8, 128), F32),
            pltpu.VMEM((MEM, 8, 128), F32),
            pltpu.VMEM((8, 128), F32),
            pltpu.VMEM((TILES, 8, 128), F32),
            dma((NZ,)), dma((NZ,)),
            dma((NZ, 2)), dma((NZ, 2)),
            dma((NZ, 2)), dma((NZ, 2)),
            dma((NZ, 2)), dma((NZ, 2)),
            dma((NZ,)), dma((NZ,)),
            dma(()),
            dma((GRP,)), dma((GRP,)),
            dma((GRP,)), dma((GRP,)),
            dma((TILES,)), dma((MEM,)),
            dma((MEM,)), dma((TILES,)),
            dma((GRP,)), dma((GRP,)),
        ],
        compiler_params=pltpu.CompilerParams(collective_id=0, has_side_effects=True),
    )(
        src_tile[0, 0].T,
        dst_tile[0, 0].T,
        tile_count,
        features.reshape(2, 2, 2, 2, share, width),
        patterns.reshape(2, NZ, slots, tile, tile),
        cotangent,
        w_self,
        w_neigh,
        bias.reshape(1, width),
    )
    layer, grad_self, grad_neigh, grad_bias = pl.pallas_call(
        pack_kernel,
        out_shape=(
            jax.ShapeDtypeStruct((share, width), F32),
            jax.ShapeDtypeStruct((width, width), F32),
            jax.ShapeDtypeStruct((width, width), F32),
            jax.ShapeDtypeStruct((1, width), F32),
        ),
        in_specs=[vmem] * 3,
        out_specs=(vmem,) * 4,
    )(layer, tiles, bias_tile)
    return layer, grad_self, grad_neigh, grad_bias.reshape(width)


def solution(mesh):
    placed = (
        P("mem", None),
        P("grp", "mem", None, None, None, None),
        P("grp", "mem", None, None),
        P("grp", "mem", None, None),
        P("grp", "mem"),
        P(("mem", "grp"), None),
        P(),
        P(),
        P(),
    )
    return jax.shard_map(
        on_device,
        mesh=mesh,
        in_specs=placed,
        out_specs=(P(("mem", "grp"), None), P(), P(), P()),
        check_vma=False,
    )
```

time: 162 us -> 118 us (0.73)
  Pallas kernels: 153 us -> 116 us
  local copies, waits for them, and re-layouts: 7.2 us -> 0 us
    pallas_call x3 -> x2, Pallas kernels: 153 us -> 116 us  [the longest x1 114 us: on_device(): pl.pallas_call(kernel, out_shape=(jax.ShapeDtypeStruct((share, width), F3...]
    unnamed x3 -> x0, local copies, waits for them, and re-layouts: 2.87 us -> none
    reshape x3 -> x0, local copies, waits for them, and re-layouts: 2.48 us -> none  [the longest x1 1.25 us: tail(): return (layer, full[0], full[1], bias_tile[:2].reshape(width))]
    squeeze x1 -> x0, local copies, waits for them, and re-layouts: 1.85 us -> none  [tail(): return (layer, full[0], full[1], bias_tile[:2].reshape(width))]
where the time goes in v2:
time: 118 us; the launch traced here: 117 us
  Pallas kernels  116 us (98%)
  between operations  1.29 us (1%)
    pallas_call x1, Pallas kernels, on_device(): pl.pallas_call(kernel, out_shape=(jax.ShapeDtypeStruct((share, width), F3...  114 us

profile of v2, /device:TPU:1, one launch (start us, length us, event | category | flops | bytes accessed | tf_op | source)
XLA Modules:
  0.0 117.4 jit_solution(12094364055268336684)
XLA Ops:
  1.3 114.2 %shard_map.120 = (f32[24,256]{1,0:T(8,128)}, f32[16,8,8,128]{3,2,1,0:T(8,128)}, f32[8,128]{1,0:T(8,128)}) custom-call(s32[2,32]{1,0:T(2,128)} %bitcast.12, s32[2,32]{1,0:T(2,128)} %bitcast.13, s32[1,1]{1,0:T(1,128)S(6)} %copy.13.cnt_ref, f32[2,2,2,2,24,256]{5,4,3,2,1,0:T(8,128)} %bitcast.11, bf16[2,16,2,128,128]{4,3,2,1,0:T(8,128)(2,1)} %bitcast.10, ...), custom_call_target="tpu_custom_call" | custom-call | tf_op jit(solution)/shard_map/pallas_call | solution.py:378
  115.5 1.9 %shard_map.121 = (f32[24,256]{1,0:T(8,128)}, f32[256,256]{1,0:T(8,128)}, f32[256,256]{1,0:T(8,128)}, f32[1,256]{1,0:T(1,128)}) custom-call(f32[24,256]{1,0:T(8,128)} %get-tuple-element.11.layer_ref, f32[16,8,8,128]{3,2,1,0:T(8,128)} %get-tuple-element.12.tiles_ref, f32[8,128]{1,0:T(8,128)} %get-tuple-element.13.bias_ref), custom_call_target="tpu_custom_call" | custom-call | tf_op jit(solution)/shard_map/pallas_call | solution.py:424

commit v3 on v2

--- a/solution.py
+++ b/solution.py
@@ -25,10 +25,10 @@
 
 
 def kernel(
-    src_ref, dst_ref, cnt_ref, f_ref, w_ref, cot_ref, ws_ref, wn_ref, b_ref,
+    src_ref, dst_ref, cnt_ref, f_ref, w_ref, rows_ref, cot_ref, ws_ref, wn_ref, b_ref,
     layer_ref, grad_ref, bias_ref,
     g_ref, pair_ref, acc_ref, deg_ref, u_ref, r1, part, r2, mine, r3, total, fin,
-    zs, zr, ys, yr, fs, fr, xs, xr, cs, cr, own_sem,
+    zs, zr, es, er, ys, yr, fs, fr, xs, xr, cs, cr, own_sem,
     s1, q1, s2, q2, s3, q3, s4, q4, s5, q5,
 ):
     g = lax.axis_index("grp")
@@ -38,7 +38,7 @@
     y = (m // NZ) * 2 + g // (2 * NX)
     z = m % NZ
     xp = x % 2
-    share, width = f_ref.shape[-2:]
+    share, width = rows_ref.shape[-2:]
     block = GRP * share
     slots, tile = w_ref.shape[2], w_ref.shape[3]
     tblocks = block // tile
@@ -47,7 +47,11 @@
         return ((y_ % 2) * NX + x_) * 2 + c_, (y_ // 2) * NZ + z_
 
     right_z, left_z = (z + 1) % NZ, (z + NZ - 1) % NZ
-    right_y, left_y = (y + 1) % NY, (y + NY - 1) % NY
+    near_y, far_y = y + 1 - 2 * (y % 2), NY - 1 - y
+
+    def place(y_):
+        return jnp.where((y_ == 1) | (y_ == 2), 1 + y_, y_ // 3)
+
     right_x, left_x = (x + 1) % NX, (x + NX - 1) % NX
 
     barrier = pltpu.get_barrier_semaphore()
@@ -56,45 +60,41 @@
         pl.semaphore_signal(barrier, inc=1, device_id=((g + k) % GRP, m), device_id_type=MESH)
         return carry
 
-    def greet_mem(k, carry):
-        pl.semaphore_signal(barrier, inc=1, device_id=(g, (m + k) % MEM), device_id_type=MESH)
-        return carry
-
-    for peer in (dev(x, right_y, z, core), dev(x, left_y, z, core)):
+    for peer in (dev(x, far_y, z, core), dev(x, y, right_z, core), dev(x, y, left_z, core)):
         pl.semaphore_signal(barrier, inc=1, device_id=peer, device_id_type=MESH)
     lax.fori_loop(1, GRP, greet_grp, 0)
-    lax.fori_loop(1, MEM, greet_mem, 0)
-    pl.semaphore_wait(barrier, GRP + MEM)
+    pl.semaphore_wait(barrier, GRP + 2)
 
     def z_of(q):
         t = (q + 1) // 2
         return jnp.where(q % 2 == 1, z + NZ - t, z + t) % NZ
 
     def piece(q, y_):
-        return g_ref.at[z_of(q), core, xp, :, y_]
-
-    own_part = f_ref.at[core, xp, :, y % 2]
+        return g_ref.at[z_of(q), core, pl.ds(xp, 2), :, place(y_)]
+
+    own_part = f_ref.at[core, pl.ds(xp, 2), :, y % 2]
     local = pltpu.make_async_copy(own_part, piece(0, y), own_sem)
     local.start()
+    trade = remote(own_part, piece(0, y), es, er, dev(x, far_y, z, core))
+    trade.start()
     acc_ref[...] = jnp.zeros_like(acc_ref)
     deg_ref[...] = jnp.zeros_like(deg_ref)
     local.wait()
 
-    def z_copy(q, to, slot):
-        return remote(piece(q, y), piece(q, y), zs.at[slot], zr.at[slot], dev(x, y, to, core))
-
-    def near(q, side):
-        to = right_y if side == 0 else left_y
-        return remote(piece(q, y), piece(q, y), ys.at[q, side], yr.at[q, side], dev(x, to, z, core))
-
-    def far(q, side):
-        came, to = (left_y, right_y) if side == 0 else (right_y, left_y)
-        half = g_ref.at[z_of(q), core, xp, side, came]
-        return remote(half, half, fs.at[q, side], fr.at[q, side], dev(x, to, z, core))
+    def z_copy(q, to, slot, which):
+        part_ = piece(q, y if which == 0 else far_y)
+        return remote(part_, part_, zs.at[slot, which], zr.at[slot, which], dev(x, y, to, core))
+
+    def near(q):
+        return remote(piece(q, y), piece(q, y), ys.at[q], yr.at[q], dev(x, near_y, z, core))
+
+    def far(q):
+        came = piece(q, near_y)
+        return remote(came, came, fs.at[q], fr.at[q], dev(x, far_y, z, core))
 
     def cross(q, side):
         to = right_x if side == 0 else left_x
-        half = g_ref.at[z_of(q), core, xp, side]
+        half = g_ref.at[z_of(q), core, 2 * xp, side]
         return remote(half, half, xs.at[q, side], xr.at[q, side], dev(to, y, z, core))
 
     def swap(q):
@@ -106,7 +106,10 @@
         add = None
         deg = None
         for yhi in range(2):
-            rows = g_ref[zq, :, :, :, yhi * 2 : yhi * 2 + 2].reshape(block, width)
+            low, high = (0, 2) if yhi == 0 else (3, 1)
+            rows = jnp.stack(
+                [g_ref[zq, :, :, :, low], g_ref[zq, :, :, :, high]], axis=3
+            ).reshape(block, width)
             hi = rows.astype(jnp.bfloat16)
             lo = (rows - hi.astype(F32)).astype(jnp.bfloat16)
             for s in range(tblocks):
@@ -140,36 +143,37 @@
         def _():
             q = i
 
-            @pl.when(q == 0)
-            def _():
-                z_copy(q, right_z, 1).start()
-                z_copy(q, left_z, 2).start()
-
-            @pl.when(q > 0)
-            def _():
-                z_copy(q, right_z, q).wait_recv()
-
-                @pl.when(q + 2 < NZ)
+            for which in range(2):
+                @pl.when(q == 0)
                 def _():
-                    z_copy(q, jnp.where(q % 2 == 1, right_z, left_z), q + 2).start()
-
-            near(q, 0).start()
-            near(q, 1).start()
+                    if which == 1:
+                        trade.wait_recv()
+                    z_copy(q, right_z, 1, which).start()
+                    z_copy(q, left_z, 2, which).start()
+
+                @pl.when(q > 0)
+                def _():
+                    z_copy(q, right_z, q, which).wait_recv()
+
+                    @pl.when(q + 2 < NZ)
+                    def _():
+                        to = jnp.where(q % 2 == 1, right_z, left_z)
+                        z_copy(q, to, q + 2, which).start()
+
+                if which == 0:
+                    near(q).start()
 
         @pl.when(within(i, LAG))
         def _():
             q = i - LAG
-            near(q, 0).wait_recv()
-            far(q, 0).start()
-            near(q, 1).wait_recv()
-            far(q, 1).start()
+            near(q).wait_recv()
+            far(q).start()
 
         @pl.when(within(i, 2 * LAG))
         def _():
             q = i - 2 * LAG
-            far(q, 0).wait_recv()
+            far(q).wait_recv()
             cross(q, 0).start()
-            far(q, 1).wait_recv()
             cross(q, 1).start()
 
         @pl.when(within(i, 3 * LAG))
@@ -225,17 +229,19 @@
     def drain(q, carry):
         @pl.when(q > 0)
         def _():
-            z_copy(q, right_z, q).wait_send()
-
+            for which in range(2):
+                z_copy(q, right_z, q, which).wait_send()
+
+        near(q).wait_send()
+        far(q).wait_send()
         for side in range(2):
-            near(q, side).wait_send()
-            far(q, side).wait_send()
             cross(q, side).wait_send()
         swap(q).wait_send()
         return carry
 
+    trade.wait_send()
     lax.fori_loop(0, NZ, drain, 0)
-    own = f_ref[g // 8, (g // 4) % 2, (g // 2) % 2, g % 2]
+    own = rows_ref[g]
     pre = jnp.dot(own, ws_ref[...], precision=HIGH, preferred_element_type=F32) + b_ref[...]
     end_grp(send_sum)
     whole = u_ref[g]
@@ -382,10 +388,10 @@
             jax.ShapeDtypeStruct((GRP, 8, 8, 128), F32),
             jax.ShapeDtypeStruct((8, 128), F32),
         ),
-        in_specs=[smem] * 3 + [vmem] * 6,
+        in_specs=[smem] * 3 + [vmem] * 7,
         out_specs=(vmem, vmem, vmem),
         scratch_shapes=[
-            pltpu.VMEM((NZ, 2, 2, 2, NY, share, width), F32),
+            pltpu.VMEM((NZ, 2, 3, 2, NY, block // 24, width), F32),
             pltpu.VMEM((2, tblocks, 2 * tile, width), jnp.bfloat16),
             pltpu.VMEM((block, width), F32),
             pltpu.VMEM((block, tile), F32),
@@ -397,9 +403,10 @@
             pltpu.VMEM((MEM, 8, 128), F32),
             pltpu.VMEM((8, 128), F32),
             pltpu.VMEM((TILES, 8, 128), F32),
+            dma((NZ, 2)), dma((NZ, 2)),
+            dma(()), dma(()),
             dma((NZ,)), dma((NZ,)),
-            dma((NZ, 2)), dma((NZ, 2)),
-            dma((NZ, 2)), dma((NZ, 2)),
+            dma((NZ,)), dma((NZ,)),
             dma((NZ, 2)), dma((NZ, 2)),
             dma((NZ,)), dma((NZ,)),
             dma(()),
@@ -414,8 +421,9 @@
         src_tile[0, 0].T,
         dst_tile[0, 0].T,
         tile_count,
-        features.reshape(2, 2, 2, 2, share, width),
+        features.reshape(2, 3, 2, 2, block // 24, width),
         patterns.reshape(2, NZ, slots, tile, tile),
+        features.reshape(GRP, share, width),
         cotangent,
         w_self,
         w_neigh,

time: 118 us -> 114 us (0.966)
  Pallas kernels: 116 us -> 113 us
    pallas_call x1, Pallas kernels: 114 us -> 111 us  [on_device(): pl.pallas_call(kernel, out_shape=(jax.ShapeDtypeStruct((share, width), F3...]
where the time goes in v3:
time: 114 us
  Pallas kernels  113 us (99%)
  between operations  1.29 us (1%)
    pallas_call x1, Pallas kernels, on_device(): pl.pallas_call(kernel, out_shape=(jax.ShapeDtypeStruct((share, width), F3...  111 us

profile of v3, /device:TPU:1, one launch (start us, length us, event | category | flops | bytes accessed | tf_op | source)
XLA Modules:
  0.0 114.2 jit_solution(15925284041483368613)
XLA Ops:
  1.3 111.1 %shard_map.120 = (f32[24,256]{1,0:T(8,128)}, f32[16,8,8,128]{3,2,1,0:T(8,128)}, f32[8,128]{1,0:T(8,128)}) custom-call(s32[2,32]{1,0:T(2,128)} %bitcast.14, s32[2,32]{1,0:T(2,128)} %bitcast.15, s32[1,1]{1,0:T(1,128)S(6)} %copy.13.cnt_ref, f32[2,3,2,2,16,256]{5,4,3,2,1,0:T(8,128)} %bitcast.12, bf16[2,16,2,128,128]{4,3,2,1,0:T(8,128)(2,1)} %bitcast.11, ...), custom_call_target="tpu_custom_call" | custom-call | tf_op jit(solution)/shard_map/pallas_call | solution.py:384
  112.3 1.9 %shard_map.121 = (f32[24,256]{1,0:T(8,128)}, f32[256,256]{1,0:T(8,128)}, f32[256,256]{1,0:T(8,128)}, f32[1,256]{1,0:T(1,128)}) custom-call(f32[24,256]{1,0:T(8,128)} %get-tuple-element.11.layer_ref, f32[16,8,8,128]{3,2,1,0:T(8,128)} %get-tuple-element.12.tiles_ref, f32[8,128]{1,0:T(8,128)} %get-tuple-element.13.bias_ref), custom_call_target="tpu_custom_call" | custom-call | tf_op jit(solution)/shard_map/pallas_call | solution.py:432

commit v4 on v2

--- a/solution.py
+++ b/solution.py
@@ -56,15 +56,10 @@
         pl.semaphore_signal(barrier, inc=1, device_id=((g + k) % GRP, m), device_id_type=MESH)
         return carry
 
-    def greet_mem(k, carry):
-        pl.semaphore_signal(barrier, inc=1, device_id=(g, (m + k) % MEM), device_id_type=MESH)
-        return carry
-
-    for peer in (dev(x, right_y, z, core), dev(x, left_y, z, core)):
+    for peer in (dev(x, NY - 1 - y, z, core), dev(x, y, right_z, core), dev(x, y, left_z, core)):
         pl.semaphore_signal(barrier, inc=1, device_id=peer, device_id_type=MESH)
     lax.fori_loop(1, GRP, greet_grp, 0)
-    lax.fori_loop(1, MEM, greet_mem, 0)
-    pl.semaphore_wait(barrier, GRP + MEM)
+    pl.semaphore_wait(barrier, GRP + 2)
 
     def z_of(q):
         t = (q + 1) // 2
@@ -312,11 +307,20 @@
         total[...] = acc
         fin[mine_k] = acc
 
-        def give(k, carry):
-            hand_out(k).start()
+        def give(t, carry):
+            d = NZ // 2 - t
+            hand_out(d).start()
+            hand_out(NZ + d).start()
+
+            @pl.when(t > 0)
+            def _():
+                hand_out(NZ - d).start()
+                hand_out(2 * NZ - d).start()
+
             return carry
 
-        lax.fori_loop(1, MEM, give, 0)
+        lax.fori_loop(0, NZ // 2, give, 0)
+        hand_out(NZ).start()
 
     def take_tile(k, carry):
         @pl.when(owner_of(k) != m)

time: 118 us -> 113 us (0.958)
  Pallas kernels: 116 us -> 111 us
    pallas_call x1, Pallas kernels: 114 us -> 109 us  [on_device(): pl.pallas_call(kernel, out_shape=(jax.ShapeDtypeStruct((share, width), F3...]
where the time goes in v4:
time: 113 us; the launch traced here: 112 us
  Pallas kernels  111 us (98%)
  between operations  1.29 us (1%)
    pallas_call x1, Pallas kernels, on_device(): pl.pallas_call(kernel, out_shape=(jax.ShapeDtypeStruct((share, width), F3...  109 us

profile of v4, /device:TPU:1, one launch (start us, length us, event | category | flops | bytes accessed | tf_op | source)
XLA Modules:
  0.0 112.5 jit_solution(11600559640119999657)
XLA Ops:
  1.3 109.3 %shard_map.120 = (f32[24,256]{1,0:T(8,128)}, f32[16,8,8,128]{3,2,1,0:T(8,128)}, f32[8,128]{1,0:T(8,128)}) custom-call(s32[2,32]{1,0:T(2,128)} %bitcast.12, s32[2,32]{1,0:T(2,128)} %bitcast.13, s32[1,1]{1,0:T(1,128)S(6)} %copy.13.cnt_ref, f32[2,2,2,2,24,256]{5,4,3,2,1,0:T(8,128)} %bitcast.11, bf16[2,16,2,128,128]{4,3,2,1,0:T(8,128)(2,1)} %bitcast.10, ...), custom_call_target="tpu_custom_call" | custom-call | tf_op jit(solution)/shard_map/pallas_call | solution.py:382
  110.6 1.9 %shard_map.121 = (f32[24,256]{1,0:T(8,128)}, f32[256,256]{1,0:T(8,128)}, f32[256,256]{1,0:T(8,128)}, f32[1,256]{1,0:T(1,128)}) custom-call(f32[24,256]{1,0:T(8,128)} %get-tuple-element.11.layer_ref, f32[16,8,8,128]{3,2,1,0:T(8,128)} %get-tuple-element.12.tiles_ref, f32[8,128]{1,0:T(8,128)} %get-tuple-element.13.bias_ref), custom_call_target="tpu_custom_call" | custom-call | tf_op jit(solution)/shard_map/pallas_call | solution.py:428
